TPU v7x, 32 devices: a whole 2x2x4 slice. The times are simulated.
32 devices in a mesh: row: 8 (over z, x), col: 4 (over y, core).
Axes of the slice: x: 2, y: 2, z: 4, core: 2. Of those that a mesh axis runs over, the one named last changes fastest.
Arguments:
- alignment: bfloat16 [256, 192, 256], P('row', 'col'), may hold values from -8 to 8
- alignment_mask: int32 [256, 192], P('row', 'col'), may hold values from 0 to 1, as said below
- residue_mask: int32 [192], replicated, may hold values from 0 to 1, as said below
- pair_features: bfloat16 [192, 192, 128], P('row', 'col'), may hold values from -6 to 6
- outer_product_left: bfloat16 [256, 32], replicated, may hold values from -0.375 to 0.375
- outer_product_right: bfloat16 [256, 32], replicated, may hold values from -0.375 to 0.375
- outer_proj: bfloat16 [1024, 128], replicated, may hold values from -0.1875 to 0.1875
- triangle_proj: bfloat16 [128, 512], replicated, may hold values from -0.5 to 0.5
- triangle_gate: bfloat16 [128, 128], replicated, may hold values from -0.5 to 0.5
- triangle_out: bfloat16 [128, 128], replicated, may hold values from -0.5 to 0.5
- transition_in: bfloat16 [128, 512], replicated, may hold values from -0.5 to 0.5
- transition_out: bfloat16 [512, 128], replicated, may hold values from -0.25 to 0.25
Outputs:
- pair_out: bfloat16 [192, 192, 128], P('row', 'col')
Inputs may be any that keep to these rules, and one draw needn't show every extreme that they name: `residue_mask`: masked residues scattered anywhere; at least one residue is masked and at least one takes part. `alignment_mask`: 0 wherever residue_mask is 0.
All inputs are finite; a program needn't handle non-finite values.
Results may differ from a plain program's by a relative error of at most 0.014.
Values may be sent and summed in bfloat16 or wider, within the bound.
No kernel may reach another device: no remote copies, remote signals or barrier semaphores. Data moves between devices by JAX's collectives and lax.ppermute only.
A program may use at most 64 MiB of HBM per device.

v0:
```python
import jax
import jax.numpy as jnp
from jax import lax
from jax.sharding import PartitionSpec as P

epsilon = 1e-05


def normalize(values):
    mean_value = jnp.mean(values, axis=-1, keepdims=True)
    centered = values - mean_value
    variance = jnp.mean(centered * centered, axis=-1, keepdims=True)
    return centered * lax.rsqrt(variance + epsilon)


def shards(
    alignment,
    alignment_mask,
    residue_mask,
    pair_features,
    outer_product_left,
    outer_product_right,
    outer_proj,
    triangle_proj,
    triangle_gate,
    triangle_out,
    transition_in,
    transition_out,
):
    block_rows, block_cols, channels = pair_features.shape
    inner = triangle_out.shape[0]
    narrow = outer_product_left.shape[1]
    mask_float = alignment_mask.astype(jnp.float32)
    normed = normalize(alignment.astype(jnp.float32)).astype(jnp.bfloat16)
    left_side = (
        jnp.dot(normed, outer_product_left, preferred_element_type=jnp.float32)
        * mask_float[..., None]
    ).astype(jnp.bfloat16)
    right_side = (
        jnp.dot(normed, outer_product_right, preferred_element_type=jnp.float32)
        * mask_float[..., None]
    ).astype(jnp.bfloat16)
    mask_wire = alignment_mask.astype(jnp.bfloat16)
    right_all, right_mask = (
        lax.all_gather(right_side, "row", axis=0, tiled=True),
        lax.all_gather(mask_wire, "row", axis=0, tiled=True),
    )
    left_rows, left_row_mask = (
        lax.all_gather(left_side, "col", axis=1, tiled=True),
        lax.all_gather(mask_wire, "col", axis=1, tiled=True),
    )
    left_all, left_mask = (
        lax.all_to_all(left_rows, "row", split_axis=1, concat_axis=0, tiled=True),
        lax.all_to_all(left_row_mask, "row", split_axis=1, concat_axis=0, tiled=True),
    )
    sequences = left_all.shape[0]
    contract = (((0,), (0,)), ((), ()))
    outer = lax.dot_general(
        left_all.reshape(sequences, block_rows * narrow),
        right_all.reshape(sequences, block_cols * narrow),
        contract,
        preferred_element_type=jnp.float32,
    )
    outer = (
        outer.reshape(block_rows, narrow, block_cols, narrow)
        .transpose(0, 2, 1, 3)
        .astype(jnp.bfloat16)
    )
    outer = outer.reshape(block_rows, block_cols, narrow * narrow)
    projected = jnp.dot(outer, outer_proj, preferred_element_type=jnp.float32)
    counts = lax.dot_general(left_mask, right_mask, contract, preferred_element_type=jnp.float32)
    first = (
        pair_features.astype(jnp.float32) + projected / jnp.maximum(counts, 1.0)[..., None]
    ).astype(jnp.bfloat16)
    normed_pair = normalize(first.astype(jnp.float32)).astype(jnp.bfloat16)
    projections = jnp.dot(normed_pair, triangle_proj, preferred_element_type=jnp.float32)
    row_mask = lax.dynamic_slice_in_dim(
        residue_mask, lax.axis_index("row") * block_rows, block_rows
    ).astype(jnp.float32)
    col_mask = lax.dynamic_slice_in_dim(
        residue_mask, lax.axis_index("col") * block_cols, block_cols
    ).astype(jnp.float32)
    pair_mask = (row_mask[:, None] * col_mask[None, :])[..., None]
    left_tri = (
        jax.nn.sigmoid(projections[..., :inner]) * projections[..., inner : 2 * inner] * pair_mask
    ).astype(jnp.bfloat16)
    right_tri = (
        jax.nn.sigmoid(projections[..., 2 * inner : 3 * inner])
        * projections[..., 3 * inner :]
        * pair_mask
    ).astype(jnp.bfloat16)
    right_cols = lax.all_gather(right_tri, "row", axis=0, tiled=True)
    right_rows = lax.all_to_all(right_cols, "col", split_axis=0, concat_axis=1, tiled=True)
    summed = jnp.einsum(
        "ikc,jkc->ijc",
        lax.all_gather(left_tri, "col", axis=1, tiled=True),
        right_rows,
        preferred_element_type=jnp.float32,
    )
    normed_sum = normalize(summed).astype(jnp.bfloat16)
    update = jax.nn.sigmoid(
        jnp.dot(normed_pair, triangle_gate, preferred_element_type=jnp.float32)
    ) * jnp.dot(normed_sum, triangle_out, preferred_element_type=jnp.float32)
    second = (first.astype(jnp.float32) + update).astype(jnp.bfloat16)
    normed_second = normalize(second.astype(jnp.float32)).astype(jnp.bfloat16)
    hidden_units = jnp.maximum(
        jnp.dot(normed_second, transition_in, preferred_element_type=jnp.float32), 0.0
    ).astype(jnp.bfloat16)
    return (
        second.astype(jnp.float32)
        + jnp.dot(hidden_units, transition_out, preferred_element_type=jnp.float32)
    ).astype(jnp.bfloat16)


def solution(mesh):
    placed = (
        P("row", "col", None),
        P("row", "col"),
        P(),
        P("row", "col", None),
        P(),
        P(),
        P(),
        P(),
        P(),
        P(),
        P(),
        P(),
    )
    return jax.shard_map(
        shards, mesh=mesh, in_specs=placed, out_specs=P("row", "col", None), check_vma=False
    )
```

profile of v0, /device:TPU:0, one launch (start us, length us, event | category | flops | bytes accessed | tf_op | source)
XLA Modules:
  0.0 276.2 jit_solution(16021958013082864905)
XLA Ops:
  6.5 0.0 copy-start
  6.5 0.8 fusion.48
  7.4 6.2 %all-gather = bf16[4,48,32]{1,2,0:T(8,128)(2,1)S(1)} all-gather(bf16[1,48,32]{1,2,0:T(8,128)(2,1)S(1)} %bitcast.93), channel_id=1, replica_groups=mesh['row'=8,'col'=4] {'col'}, dimensions={0}, use_global_device_ids=true | all-gather | bytes 15360 | tf_op jit(solution)/shard_map/all_gather | solution.py:50
  13.6 0.1 reshape.97
  13.7 0.1 copy.69
  13.8 0.7 reshape.110
  14.5 6.2 %all-to-all-start.1 = ((bf16[8,2,384]{2,1,0:T(2,128)(2,1)}), bf16[8,2,384]{2,1,0:T(2,128)(2,1)S(1)}, u32[]{:S(2)}, u32[]{:S(2)}) async-start(bf16[8,2,384]{2,1,0:T(2,128)(2,1)} %reshape.110), calls=%async_computation.1 | async-start | bytes 24576 | tf_op jit(solution)/shard_map/all_to_all | solution.py:54
  20.8 1.4 convert_reduce_fusion
  22.2 0.5 fusion.2
  22.7 0.7 fusion.16
  23.4 0.0 copy-start.12
  23.4 0.6 copy.51
  24.1 13.4 %all_gather.18 = bf16[32,192,32]{2,0,1:T(8,128)(2,1)} all-gather(bf16[32,48,32]{2,0,1:T(8,128)(2,1)S(1)} %copy.51), channel_id=1, replica_groups=mesh['row'=8,'col'=4] {'col'}, dimensions={1}, use_global_device_ids=true | all-gather | bytes 491520 | tf_op jit(solution)/shard_map/all_gather | solution.py:49
  37.4 0.7 fusion.17
  38.1 0.0 copy-start.13
  38.1 45.3 %all_gather.19 = bf16[256,48,32]{1,2,0:T(8,128)(2,1)S(1)} all-gather(bf16[32,48,32]{1,2,0:T(8,128)(2,1)S(1)} %fusion.17), channel_id=1, replica_groups=mesh['row'=8,'col'=4] {'row'}, dimensions={0}, use_global_device_ids=true | all-gather | bytes 884736 | tf_op jit(solution)/shard_map/all_gather | solution.py:45
  83.4 0.1 dynamic-slice_convert_fusion.1
  83.5 0.1 dynamic-slice_convert_fusion
  83.6 3.8 %reshape.108 = bf16[8,2,12288]{2,1,0:T(2,128)(2,1)} reshape(bf16[192,32,32]{2,1,0:T(8,128)(2,1)} %bitcast.89) | data formatting | bytes 786432
  87.4 2.4 copy.56
  89.8 0.0 all-to-all-done.1
  89.8 3.6 %all-to-all-start = ((bf16[8,2,12288]{2,1,0:T(2,128)(2,1)}), bf16[8,2,12288]{2,1,0:T(2,128)(2,1)S(1)}, u32[]{:S(2)}, u32[]{:S(2)}) async-start(bf16[8,2,12288]{2,1,0:T(2,128)(2,1)} %reshape.108), calls=%async_computation | async-start | bytes 786432 | tf_op jit(solution)/shard_map/all_to_all | solution.py:53
  93.4 0.0 all-gather.4.cloned.1.call-start
  93.4 35.2 %all_gather.21 = bf16[256,48]{1,0:T(8,128)(2,1)S(1)} all-gather(bf16[32,48]{1,0:T(8,128)(2,1)S(1)} %get-tuple-element.7), channel_id=1, replica_groups=mesh['row'=8,'col'=4] {'row'}, dimensions={0}, use_global_device_ids=true | all-gather | bytes 27648 | tf_op jit(solution)/shard_map/all_gather | solution.py:46
  128.6 0.1 broadcast_multiply_fusion.1
  128.7 0.1 reshape.111
  128.8 0.1 all_to_all.44
  128.9 0.1 convolution_maximum_fusion
  129.0 0.0 all-to-all-done
  129.0 0.8 reshape.109
  129.8 0.6 copy.53
  130.4 1.0 reshape.93
  131.4 0.2 copy.54
  131.6 3.7 %convert_bitcast_fusion = bf16[24,48,32,32]{1,2,3,0:T(8,128)(2,1)} fusion(bf16[24,32,256,1]{2,1,3,0:T(8,128)(2,1)S(1)} %bitcast.90, bf16[48,32,256]{2,0,1:T(8,128)(2,1)S(1)} %copy-done.4), kind=kOutput, calls=%fused_computation | convolution fusion | flops 605159424 | bytes 3538944 | tf_op jit(solution)/shard_map/dot_general | solution.py:58
  135.3 17.8 %copy.57 = bf16[24,48,32,32]{3,2,1,0:T(8,128)(2,1)} copy(bf16[24,48,32,32]{1,2,3,0:T(8,128)(2,1)} %convert_bitcast_fusion) | data formatting | bytes 4718592 | tf_op jit(solution)/shard_map/convert_element_type | solution.py:67
  153.1 12.7 %reshape.95 = bf16[24,48,1024]{2,1,0:T(8,128)(2,1)S(1)} reshape(bf16[24,48,32,32]{3,2,1,0:T(8,128)(2,1)} %copy.57) | data formatting | bytes 4718592 | tf_op jit(solution)/shard_map/reshape | solution.py:69
  165.9 0.0 copy-start.6
  165.9 1.8 fusion.49
  167.8 0.4 multiply_reduce_fusion.2
  168.2 0.5 fusion.41
  168.7 1.2 fusion.22
  169.9 0.0 all-gather.4.cloned.1.call-update
  169.9 0.0 all-gather.6.cloned.1.call-start
  170.0 0.7 all-gather.6.cloned.1.call-update
  170.7 0.0 copy-start.10
  170.7 48.0 %all-gather.4.cloned.1.call-done = bf16[192,48,128]{2,1,0:T(8,128)(2,1)} async-done(((bf16[24,48,128]{2,1,0:T(8,128)(2,1)}), bf16[192,48,128]{2,1,0:T(8,128)(2,1)}) %all-gather.4.cloned.1.call-update) | async-done | bytes 2359312 | tf_op jit(solution)/shard_map/all_gather | solution.py:92
  218.7 3.9 %all-to-all-start.2 = ((bf16[192,48,128]{2,1,0:T(8,128)(2,1)}), bf16[192,48,128]{2,1,0:T(8,128)(2,1)S(1)}, u32[]{:S(2)}, u32[]{:S(2)}) async-start(bf16[192,48,128]{2,1,0:T(8,128)(2,1)} %all-gather.4.cloned.1.call-done), calls=%async_computation.2 | async-start | bytes 4718592 | tf_op jit(solution)/shard_map/all_to_all | solution.py:93
  222.6 1.3 fusion.9
  223.9 18.8 %all-gather.6.cloned.1.call-done = bf16[24,192,128]{2,1,0:T(8,128)(2,1)} async-done(((bf16[24,48,128]{2,1,0:T(8,128)(2,1)}), bf16[24,192,128]{2,1,0:T(8,128)(2,1)}) %all-gather.6.cloned.1.call-update) | async-done | bytes 1179664 | tf_op jit(solution)/shard_map/all_gather | solution.py:96
  242.7 2.8 %copy.63 = bf16[24,192,128]{1,0,2:T(8,128)(2,1)} copy(bf16[24,192,128]{2,1,0:T(8,128)(2,1)} %all-gather.6.cloned.1.call-done) | data formatting | bytes 2359296 | tf_op jit(solution)/shard_map/all_gather | solution.py:96
  245.5 11.6 %all-to-all-done.2 = bf16[192,48,128]{2,1,0:T(8,128)(2,1)S(1)} async-done(((bf16[192,48,128]{2,1,0:T(8,128)(2,1)}), bf16[192,48,128]{2,1,0:T(8,128)(2,1)S(1)}, u32[]{:S(2)}, u32[]{:S(2)}) %all-to-all-start.2) | async-done | bytes 2359328 | tf_op jit(solution)/shard_map/all_to_all | solution.py:93
  257.1 2.1 copy.61
  259.2 3.8 %copy.62 = bf16[48,192,128]{1,0,2:T(8,128)(2,1)S(1)} copy(bf16[48,192,128]{2,1,0:T(8,128)(2,1)} %bitcast.86) | data formatting | bytes 4718592 | tf_op jit(solution)/shard_map/all_to_all | solution.py:93
  263.0 2.4 bitcast_reduce_fusion
  265.4 0.3 multiply_reduce_fusion
  265.6 0.0 copy-start.7
  265.7 0.2 multiply_convert_fusion
  265.9 0.8 copy-done.2
  266.7 0.2 copy-done.5
  266.9 0.5 fusion.50
  267.4 0.4 multiply_reduce_fusion.1
  267.8 0.0 copy-done.8
  267.8 0.0 copy-done.9
  267.8 1.5 fusion.15
  (29 shorter events, 0.1 us)
Async XLA Ops:
  6.5 159.3 %copy-start = (bf16[1024,128]{1,0:T(8,128)(2,1)S(1)}, bf16[1024,128]{1,0:T(8,128)(2,1)}, u32[]{:S(2)}) copy-start(bf16[1024,128]{1,0:T(8,128)(2,1)} %param.18) | copy-start | bytes 786436
  6.5 15.7 %copy-start.3 = (bf16[32,48,256]{2,1,0:T(8,128)(2,1)S(1)}, bf16[32,48,256]{2,1,0:T(8,128)(2,1)}, u32[]{:S(2)}) copy-start(bf16[32,48,256]{2,1,0:T(8,128)(2,1)} %param.12) | copy-start | bytes 2359300
  6.5 16.2 %copy-start.11 = (bf16[256,32]{0,1:T(8,128)(2,1)S(1)}, bf16[256,32]{0,1:T(8,128)(2,1)}, u32[]{:S(2)}) copy-start(bf16[256,32]{0,1:T(8,128)(2,1)} %param.16) | copy-start | bytes 49156
  14.5 75.3 %all-to-all-start.1 = ((bf16[8,2,384]{2,1,0:T(2,128)(2,1)}), bf16[8,2,384]{2,1,0:T(2,128)(2,1)S(1)}, u32[]{:S(2)}, u32[]{:S(2)}) async-start(bf16[8,2,384]{2,1,0:T(2,128)(2,1)} %reshape.110), calls=%async_computation.1 | async-start | bytes 24576 | tf_op jit(solution)/shard_map/all_to_all | solution.py:54
  23.4 14.0 %copy-start.12 = (bf16[256,32]{0,1:T(8,128)(2,1)S(1)}, bf16[256,32]{0,1:T(8,128)(2,1)}, u32[]{:S(2)}) copy-start(bf16[256,32]{0,1:T(8,128)(2,1)} %param.17) | copy-start | bytes 49156
  38.1 45.4 %copy-start.13 = (s32[192]{0:T(256)S(1)}, s32[192]{0:T(256)}, u32[]{:S(2)}) copy-start(s32[192]{0:T(256)} %param.14) | copy-start | bytes 2308
  89.8 39.2 %all-to-all-start = ((bf16[8,2,12288]{2,1,0:T(2,128)(2,1)}), bf16[8,2,12288]{2,1,0:T(2,128)(2,1)S(1)}, u32[]{:S(2)}, u32[]{:S(2)}) async-start(bf16[8,2,12288]{2,1,0:T(2,128)(2,1)} %reshape.108), calls=%async_computation | async-start | bytes 786432 | tf_op jit(solution)/shard_map/all_to_all | solution.py:53
  93.4 125.3 %all-gather.4.cloned.1.call-start = ((), (), s32[]{:S(2)}) async-start(), calls=%async_computation.3 | async-start | bytes 2654208 | tf_op jit(solution)/shard_map/all_gather | solution.py:92
  130.4 1.2 copy-start.4
  165.9 2.3 copy-start.6
  167.7 54.8 %copy-start.1 = (f32[24,48,128]{2,1,0:T(8,128)}, f32[24,48,128]{2,1,0:T(8,128)S(1)}, u32[]{:S(2)}) copy-start(f32[24,48,128]{2,1,0:T(8,128)S(1)} %get-tuple-element.10) | copy-start | bytes 1769476
  169.9 72.8 %all-gather.6.cloned.1.call-start = ((), (), s32[]{:S(2)}) async-start(), calls=%async_computation.4 | async-start | bytes 1474560 | tf_op jit(solution)/shard_map/all_gather | solution.py:96
  170.7 51.9 %copy-start.10 = (bf16[128,128]{1,0:T(8,128)(2,1)S(1)}, bf16[128,128]{1,0:T(8,128)(2,1)}, u32[]{:S(2)}) copy-start(bf16[128,128]{1,0:T(8,128)(2,1)} %param.20) | copy-start | bytes 98308
  218.7 38.4 %all-to-all-start.2 = ((bf16[192,48,128]{2,1,0:T(8,128)(2,1)}), bf16[192,48,128]{2,1,0:T(8,128)(2,1)S(1)}, u32[]{:S(2)}, u32[]{:S(2)}) async-start(bf16[192,48,128]{2,1,0:T(8,128)(2,1)} %all-gather.4.cloned.1.call-done), calls=%async_computation.2 | async-start | bytes 4718592 | tf_op jit(solution)/shard_map/all_to_all | solution.py:93
  265.6 1.1 copy-start.2
  265.6 1.2 copy-start.5
  265.6 1.2 copy-start.7
  266.9 0.9 copy-start.8
  266.9 1.0 copy-start.9
Sparse Core Ops, SparseCore 0:
  170.0 48.6 all-gather.3
  220.2 22.3 all-gather.5
where the time goes:
time: 277 us; the launch traced here: 276 us
  blocking collectives  100 us (36%)
  waiting for transfers between devices  79.1 us (29%)
  local copies, waits for them, and re-layouts  50.8 us (18%)
  starting transfers between devices  13.7 us (5%)
  between operations  13.7 us (5%)
  matrix products  13.2 us (5%)
  other arithmetic  5.45 us (2%)
    all_gather x1, waiting for transfers between devices, shards(): right_cols = lax.all_gather(right_tri, 'row', axis=0, tiled=True)  48 us
    all_gather x1, blocking collectives, shards(): lax.all_gather(right_side, 'row', axis=0, tiled=True)  45.3 us
    all_gather x1, blocking collectives, shards(): lax.all_gather(mask_wire, 'row', axis=0, tiled=True)  35.2 us
    all_gather x1, waiting for transfers between devices, shards(): lax.all_gather(left_tri, 'col', axis=1, tiled=True)  18.8 us
    convert_element_type x1, local copies, waits for them, and re-layouts, shards(): outer = outer.reshape(block_rows, narrow, block_cols, narrow).transpose(0...  17.8 us
    all_gather x1, blocking collectives, shards(): lax.all_gather(left_side, 'col', axis=1, tiled=True)  13.4 us
    reshape x1, local copies, waits for them, and re-layouts, shards(): outer = outer.reshape(block_rows, block_cols, narrow * narrow)  12.7 us
    all_to_all x1, waiting for transfers between devices, shards(): lax.all_to_all(right_cols, 'col', split_axis=0, concat_axis=1, tiled=True)  11.6 us
  transfers between devices with their start and end apart: 5, of which 3 were waited for; matrix products, arithmetic and copies ran while one was open for 5% of the time, Pallas kernels for 0%

commit v1 on v0

--- a/solution.py
+++ b/solution.py
@@ -90,7 +90,10 @@
         * pair_mask
     ).astype(jnp.bfloat16)
     right_cols = lax.all_gather(right_tri, "row", axis=0, tiled=True)
-    right_rows = lax.all_to_all(right_cols, "col", split_axis=0, concat_axis=1, tiled=True)
+    right_rows = jnp.concatenate(
+        lax.all_to_all(jnp.stack(jnp.split(right_cols, lax.axis_size("col"), axis=0)), "col", 0, 0),
+        axis=1,
+    )
     summed = jnp.einsum(
         "ikc,jkc->ijc",
         lax.all_gather(left_tri, "col", axis=1, tiled=True),

time: 277 us -> 281 us (1.014)
    all_gather x1, waiting for transfers between devices: 18.8 us -> 14.1 us  [shards(): lax.all_gather(left_tri, 'col', axis=1, tiled=True)]
    reshape x0 -> x1, local copies, waits for them, and re-layouts: none -> 3.78 us  [shards(): jnp.concatenate(lax.all_to_all(jnp.stack(jnp.split(right_cols, lax.axis_s...]
    all_to_all x2 -> x1, local copies, waits for them, and re-layouts: 5.89 us -> 2.13 us  [shards(): lax.all_to_all(jnp.stack(jnp.split(right_cols, lax.axis_size('col'), axis...]
    all_to_all x1, waiting for transfers between devices: 11.6 us -> 15.4 us  [shards(): lax.all_to_all(jnp.stack(jnp.split(right_cols, lax.axis_size('col'), axis...]
  transfers between devices with their start and end apart: 5 -> 5, of which waited for: 3 -> 3; matrix products, arithmetic and copies ran while one was open for 5% -> 7% of each run, Pallas kernels for 0% -> 0%
where the time goes in v1:
time: 281 us; the launch traced here: 279 us
  blocking collectives  100 us (36%)
  waiting for transfers between devices  78.2 us (28%)
  local copies, waits for them, and re-layouts  52.8 us (19%)
  starting transfers between devices  13.9 us (5%)
  between operations  13.7 us (5%)
  matrix products  13.3 us (5%)
  other arithmetic  7.17 us (3%)
    all_gather x1, waiting for transfers between devices, shards(): right_cols = lax.all_gather(right_tri, 'row', axis=0, tiled=True)  48 us
    all_gather x1, blocking collectives, shards(): lax.all_gather(right_side, 'row', axis=0, tiled=True)  45.3 us
    all_gather x1, blocking collectives, shards(): lax.all_gather(mask_wire, 'row', axis=0, tiled=True)  35.2 us
    convert_element_type x1, local copies, waits for them, and re-layouts, shards(): outer = outer.reshape(block_rows, narrow, block_cols, narrow).transpose(0...  17.8 us
    all_to_all x1, waiting for transfers between devices, shards(): lax.all_to_all(jnp.stack(jnp.split(right_cols, lax.axis_size('col'), axis...  15.4 us
    all_gather x1, waiting for transfers between devices, shards(): lax.all_gather(left_tri, 'col', axis=1, tiled=True)  14.1 us
    all_gather x1, blocking collectives, shards(): lax.all_gather(left_side, 'col', axis=1, tiled=True)  13.4 us
    reshape x1, local copies, waits for them, and re-layouts, shards(): outer = outer.reshape(block_rows, block_cols, narrow * narrow)  12.7 us
  transfers between devices with their start and end apart: 5, of which 3 were waited for; matrix products, arithmetic and copies ran while one was open for 7% of the time, Pallas kernels for 0%

profile of v1, /device:TPU:0, one launch (start us, length us, event | category | flops | bytes accessed | tf_op | source)
XLA Modules:
  0.0 279.2 jit_solution(5598558013396215464)
XLA Ops:
  6.5 0.8 fusion.48
  7.4 6.2 %all-gather = bf16[4,48,32]{1,2,0:T(8,128)(2,1)S(1)} all-gather(bf16[1,48,32]{1,2,0:T(8,128)(2,1)S(1)} %bitcast.99), channel_id=1, replica_groups=mesh['row'=8,'col'=4] {'col'}, dimensions={0}, use_global_device_ids=true | all-gather | bytes 15360 | tf_op jit(solution)/shard_map/all_gather | solution.py:50
  13.6 0.1 reshape.105
  13.7 0.1 copy.68
  13.8 0.7 reshape.118
  14.5 6.2 %all-to-all-start.1 = ((bf16[8,2,384]{2,1,0:T(2,128)(2,1)}), bf16[8,2,384]{2,1,0:T(2,128)(2,1)S(1)}, u32[]{:S(2)}, u32[]{:S(2)}) async-start(bf16[8,2,384]{2,1,0:T(2,128)(2,1)} %reshape.118), calls=%async_computation.1 | async-start | bytes 24576 | tf_op jit(solution)/shard_map/all_to_all | solution.py:54
  20.8 1.4 convert_reduce_fusion
  22.2 0.5 fusion.2
  22.7 0.7 fusion.16
  23.4 0.0 copy-start.12
  23.4 0.6 copy.50
  24.1 13.4 %all_gather.18 = bf16[32,192,32]{2,0,1:T(8,128)(2,1)} all-gather(bf16[32,48,32]{2,0,1:T(8,128)(2,1)S(1)} %copy.50), channel_id=1, replica_groups=mesh['row'=8,'col'=4] {'col'}, dimensions={1}, use_global_device_ids=true | all-gather | bytes 491520 | tf_op jit(solution)/shard_map/all_gather | solution.py:49
  37.4 0.7 fusion.17
  38.1 0.0 copy-start.13
  38.1 45.3 %all_gather.19 = bf16[256,48,32]{1,2,0:T(8,128)(2,1)S(1)} all-gather(bf16[32,48,32]{1,2,0:T(8,128)(2,1)S(1)} %fusion.17), channel_id=1, replica_groups=mesh['row'=8,'col'=4] {'row'}, dimensions={0}, use_global_device_ids=true | all-gather | bytes 884736 | tf_op jit(solution)/shard_map/all_gather | solution.py:45
  83.4 0.1 dynamic-slice_convert_fusion.1
  83.5 0.1 dynamic-slice_convert_fusion
  83.6 3.8 %reshape.116 = bf16[8,2,12288]{2,1,0:T(2,128)(2,1)} reshape(bf16[192,32,32]{2,1,0:T(8,128)(2,1)} %bitcast.95) | data formatting | bytes 786432
  87.4 2.4 copy.55
  89.8 0.0 all-to-all-done.1
  89.8 3.6 %all-to-all-start = ((bf16[8,2,12288]{2,1,0:T(2,128)(2,1)}), bf16[8,2,12288]{2,1,0:T(2,128)(2,1)S(1)}, u32[]{:S(2)}, u32[]{:S(2)}) async-start(bf16[8,2,12288]{2,1,0:T(2,128)(2,1)} %reshape.116), calls=%async_computation | async-start | bytes 786432 | tf_op jit(solution)/shard_map/all_to_all | solution.py:53
  93.4 0.0 all-gather.4.cloned.1.call-start
  93.4 35.2 %all_gather.21 = bf16[256,48]{1,0:T(8,128)(2,1)S(1)} all-gather(bf16[32,48]{1,0:T(8,128)(2,1)S(1)} %get-tuple-element.11), channel_id=1, replica_groups=mesh['row'=8,'col'=4] {'row'}, dimensions={0}, use_global_device_ids=true | all-gather | bytes 27648 | tf_op jit(solution)/shard_map/all_gather | solution.py:46
  128.6 0.1 broadcast_multiply_fusion.1
  128.7 0.1 reshape.119
  128.8 0.1 all_to_all.34
  128.9 0.1 convolution_maximum_fusion
  129.0 0.0 all-to-all-done
  129.0 0.8 reshape.117
  129.8 0.6 copy.52
  130.4 0.0 copy-start.4
  130.4 1.0 reshape.99
  131.4 0.2 copy.53
  131.6 3.7 %convert_bitcast_fusion = bf16[24,48,32,32]{1,2,3,0:T(8,128)(2,1)} fusion(bf16[24,32,256,1]{2,1,3,0:T(8,128)(2,1)S(1)} %bitcast.96, bf16[48,32,256]{2,0,1:T(8,128)(2,1)S(1)} %copy-done.4), kind=kOutput, calls=%fused_computation | convolution fusion | flops 605159424 | bytes 3538944 | tf_op jit(solution)/shard_map/dot_general | solution.py:58
  135.3 17.8 %copy.56 = bf16[24,48,32,32]{3,2,1,0:T(8,128)(2,1)} copy(bf16[24,48,32,32]{1,2,3,0:T(8,128)(2,1)} %convert_bitcast_fusion) | data formatting | bytes 4718592 | tf_op jit(solution)/shard_map/convert_element_type | solution.py:67
  153.2 12.7 %reshape.101 = bf16[24,48,1024]{2,1,0:T(8,128)(2,1)S(1)} reshape(bf16[24,48,32,32]{3,2,1,0:T(8,128)(2,1)} %copy.56) | data formatting | bytes 4718592 | tf_op jit(solution)/shard_map/reshape | solution.py:69
  165.9 0.0 copy-start.6
  165.9 1.8 fusion.49
  167.8 0.4 multiply_reduce_fusion.2
  168.2 0.5 fusion.41
  168.7 1.2 fusion.22
  169.9 0.0 all-gather.4.cloned.1.call-update
  169.9 0.0 all-gather.6.cloned.1.call-start
  170.0 0.7 all-gather.6.cloned.1.call-update
  170.7 48.0 %all-gather.4.cloned.1.call-done = bf16[192,48,128]{2,1,0:T(8,128)(2,1)} async-done(((bf16[24,48,128]{2,1,0:T(8,128)(2,1)}), bf16[192,48,128]{2,1,0:T(8,128)(2,1)}) %all-gather.4.cloned.1.call-update) | async-done | bytes 2359312 | tf_op jit(solution)/shard_map/all_gather | solution.py:92
  218.7 2.0 slice_bitcast_fusion.3
  220.7 1.7 pad_maximum_fusion
  222.4 4.0 %all-to-all-start.2 = ((bf16[4,48,48,128]{3,2,1,0:T(8,128)(2,1)}), bf16[4,48,48,128]{3,2,1,0:T(8,128)(2,1)S(1)}, u32[]{:S(2)}, u32[]{:S(2)}) async-start(bf16[4,48,48,128]{3,2,1,0:T(8,128)(2,1)} %pad_maximum_fusion), calls=%async_computation.2 | async-start | bytes 4718592 | tf_op jit(solution)/shard_map/all_to_all | solution.py:94
  226.5 1.3 fusion.9
  227.8 14.1 %all-gather.6.cloned.1.call-done = bf16[24,192,128]{2,1,0:T(8,128)(2,1)} async-done(((bf16[24,48,128]{2,1,0:T(8,128)(2,1)}), bf16[24,192,128]{2,1,0:T(8,128)(2,1)}) %all-gather.6.cloned.1.call-update) | async-done | bytes 1179664 | tf_op jit(solution)/shard_map/all_gather | solution.py:99
  241.9 2.8 copy.62
  244.7 15.4 %all-to-all-done.2 = bf16[4,48,48,128]{3,2,1,0:T(8,128)(2,1)S(1)} async-done(((bf16[4,48,48,128]{3,2,1,0:T(8,128)(2,1)}), bf16[4,48,48,128]{3,2,1,0:T(8,128)(2,1)S(1)}, u32[]{:S(2)}, u32[]{:S(2)}) %all-to-all-start.2) | async-done | bytes 2359328 | tf_op jit(solution)/shard_map/all_to_all | solution.py:94
  260.1 2.1 copy.60
  262.2 3.8 %copy.61 = bf16[48,192,128]{1,0,2:T(8,128)(2,1)S(1)} copy(bf16[48,192,128]{2,1,0:T(8,128)(2,1)} %bitcast.92) | data formatting | bytes 4718592 | tf_op jit(solution)/shard_map/reshape | solution.py:93
  266.0 2.4 bitcast_reduce_fusion
  268.4 0.3 multiply_reduce_fusion
  268.6 0.0 copy-start.7
  268.7 0.2 multiply_convert_fusion
  268.8 0.8 copy-done.2
  269.7 0.2 copy-done.5
  269.9 0.5 fusion.50
  270.4 0.4 multiply_reduce_fusion.1
  270.8 0.0 copy-done.9
  270.8 1.6 fusion.15
  (31 shorter events, 0.1 us)
Async XLA Ops:
  6.5 159.4 %copy-start = (bf16[1024,128]{1,0:T(8,128)(2,1)S(1)}, bf16[1024,128]{1,0:T(8,128)(2,1)}, u32[]{:S(2)}) copy-start(bf16[1024,128]{1,0:T(8,128)(2,1)} %param.18) | copy-start | bytes 786436
  6.5 15.7 %copy-start.3 = (bf16[32,48,256]{2,1,0:T(8,128)(2,1)S(1)}, bf16[32,48,256]{2,1,0:T(8,128)(2,1)}, u32[]{:S(2)}) copy-start(bf16[32,48,256]{2,1,0:T(8,128)(2,1)} %param.12) | copy-start | bytes 2359300
  6.5 16.2 %copy-start.11 = (bf16[256,32]{0,1:T(8,128)(2,1)S(1)}, bf16[256,32]{0,1:T(8,128)(2,1)}, u32[]{:S(2)}) copy-start(bf16[256,32]{0,1:T(8,128)(2,1)} %param.16) | copy-start | bytes 49156
  14.5 75.3 %all-to-all-start.1 = ((bf16[8,2,384]{2,1,0:T(2,128)(2,1)}), bf16[8,2,384]{2,1,0:T(2,128)(2,1)S(1)}, u32[]{:S(2)}, u32[]{:S(2)}) async-start(bf16[8,2,384]{2,1,0:T(2,128)(2,1)} %reshape.118), calls=%async_computation.1 | async-start | bytes 24576 | tf_op jit(solution)/shard_map/all_to_all | solution.py:54
  23.4 14.0 %copy-start.12 = (bf16[256,32]{0,1:T(8,128)(2,1)S(1)}, bf16[256,32]{0,1:T(8,128)(2,1)}, u32[]{:S(2)}) copy-start(bf16[256,32]{0,1:T(8,128)(2,1)} %param.17) | copy-start | bytes 49156
  38.1 45.4 %copy-start.13 = (s32[192]{0:T(256)S(1)}, s32[192]{0:T(256)}, u32[]{:S(2)}) copy-start(s32[192]{0:T(256)} %param.14) | copy-start | bytes 2308
  89.8 39.2 %all-to-all-start = ((bf16[8,2,12288]{2,1,0:T(2,128)(2,1)}), bf16[8,2,12288]{2,1,0:T(2,128)(2,1)S(1)}, u32[]{:S(2)}, u32[]{:S(2)}) async-start(bf16[8,2,12288]{2,1,0:T(2,128)(2,1)} %reshape.116), calls=%async_computation | async-start | bytes 786432 | tf_op jit(solution)/shard_map/all_to_all | solution.py:53
  93.4 125.3 %all-gather.4.cloned.1.call-start = ((), (), s32[]{:S(2)}) async-start(), calls=%async_computation.3 | async-start | bytes 2654208 | tf_op jit(solution)/shard_map/all_gather | solution.py:92
  130.4 1.2 copy-start.4
  165.9 2.3 copy-start.6
  167.8 58.7 %copy-start.1 = (f32[24,48,128]{2,1,0:T(8,128)}, f32[24,48,128]{2,1,0:T(8,128)S(1)}, u32[]{:S(2)}) copy-start(f32[24,48,128]{2,1,0:T(8,128)S(1)} %get-tuple-element.14) | copy-start | bytes 1769476
  169.9 72.0 %all-gather.6.cloned.1.call-start = ((), (), s32[]{:S(2)}) async-start(), calls=%async_computation.4 | async-start | bytes 1474560 | tf_op jit(solution)/shard_map/all_gather | solution.py:99
  222.4 4.0 %copy-start.10 = (bf16[128,128]{1,0:T(8,128)(2,1)S(1)}, bf16[128,128]{1,0:T(8,128)(2,1)}, u32[]{:S(2)}) copy-start(bf16[128,128]{1,0:T(8,128)(2,1)} %param.20) | copy-start | bytes 98308
  222.4 37.6 %all-to-all-start.2 = ((bf16[4,48,48,128]{3,2,1,0:T(8,128)(2,1)}), bf16[4,48,48,128]{3,2,1,0:T(8,128)(2,1)S(1)}, u32[]{:S(2)}, u32[]{:S(2)}) async-start(bf16[4,48,48,128]{3,2,1,0:T(8,128)(2,1)} %pad_maximum_fusion), calls=%async_computation.2 | async-start | bytes 4718592 | tf_op jit(solution)/shard_map/all_to_all | solution.py:94
  268.6 1.1 copy-start.2
  268.6 1.2 copy-start.5
  268.6 1.2 copy-start.7
  269.9 0.9 copy-start.8
  269.9 1.0 copy-start.9
Sparse Core Ops, SparseCore 0:
  170.1 48.6 all-gather.3
  220.3 21.6 all-gather.5
